TPU v7x, 512 devices: a whole 4x8x8 slice. The times are simulated.
512 devices in a mesh: row: 32 (over x, z), col: 16 (over y, core).
Axes of the slice: x: 4, y: 8, z: 8, core: 2. Of those that a mesh axis runs over, the one named last changes fastest.
Arguments:
- rhs_top: float32 [2, 32768, 2048], P(None, 'row', 'col'), may hold values from -6 to 6
- rhs_low: float32 [2, 2, 512, 2048], P(None, None, 'row', 'col'), may hold values from -6 to 6
- inv_diag: float32 [2, 2, 512, 512], P(None, None, 'row'), may hold values from -3 to 3, as said below
- coupling: float32 [2, 512, 512], P(None, 'row'), may hold values from -0.1875 to 0.1875
- panel: float32 [2, 32768, 1024], P(None, 'row', 'col'), may hold values from -0.125 to 0.125
- radiation: float32 [2, 4096, 1024], P(None, 'row'), may hold values from -0.125 to 0.125
Outputs:
- solved: float32 [2, 2, 512, 2048], P(None, None, 'row', 'col')
- updated_top: float32 [2, 32768, 2048], P(None, 'row', 'col')
- far_field: float32 [2, 4096, 2048], P(None, 'row', 'col')
Inputs may be any that keep to these rules, and one draw needn't show every extreme that they name: `inv_diag`: each of the two 512 x 512 complex blocks is upper triangular.
All inputs are finite; a program needn't handle non-finite values.
Results may differ from a plain program's by a relative error of at most 0.000094.
Values sent between devices are 32-bit elements; how exact they have to be, the bound alone decides.
No kernel may reach another device: no remote copies, remote signals or barrier semaphores. Data moves between devices by JAX's collectives and lax.ppermute only.
A program may use at most 64 MiB of HBM per device.

v0:
```python
import jax
import jax.numpy as jnp
from jax import lax
from jax.sharding import PartitionSpec as P


def plain_product(left_side, right_side):
    return jnp.dot(
        left_side, right_side, precision=lax.Precision.HIGHEST, preferred_element_type=jnp.float32
    )


def complex_product(matrix, vector):
    real_part = plain_product(matrix[0], vector[0]) - plain_product(matrix[1], vector[1])
    imag_part = plain_product(matrix[0], vector[1]) + plain_product(matrix[1], vector[0])
    return jnp.stack([real_part, imag_part], axis=0)


def apply_columns(left_side, pieces):
    return complex_product(left_side, pieces)


def local(rhs_top, rhs_low, inv_diag, coupling, panel, radiation):
    lower_part = apply_columns(inv_diag[1], lax.all_gather(rhs_low[1], "row", axis=1, tiled=True))
    lower_all = lax.all_gather(lower_part, "row", axis=1, tiled=True)
    reduced = rhs_low[0] - complex_product(coupling, lower_all)
    upper_part = apply_columns(inv_diag[0], lax.all_gather(reduced, "row", axis=1, tiled=True))
    upper_all = lax.all_gather(upper_part, "row", axis=1, tiled=True)
    currents = jnp.concatenate([upper_all, lower_all], axis=1)
    far_field = complex_product(radiation, currents)
    change = complex_product(lax.all_gather(panel, "col", axis=2, tiled=True), currents)
    updated_top = rhs_top - change
    solved = jnp.stack([upper_part, lower_part], axis=0)
    return (solved, updated_top, far_field)


def solution(mesh):
    in_specs = (
        P(None, "row", "col"),
        P(None, None, "row", "col"),
        P(None, None, "row", None),
        P(None, "row", None),
        P(None, "row", "col"),
        P(None, "row", None),
    )
    out_specs = (P(None, None, "row", "col"), P(None, "row", "col"), P(None, "row", "col"))
    return jax.shard_map(local, mesh=mesh, in_specs=in_specs, out_specs=out_specs, check_vma=False)
```

profile of v0, /device:TPU:56, one launch (start us, length us, event | category | flops | bytes accessed | tf_op | source)
XLA Modules:
  0.0 250.2 jit_solution(11060031639573226850)
XLA Ops:
  7.2 0.0 copy-start.1
  7.2 0.0 copy-start.2
  7.2 0.0 all-gather.3.cloned.1.call-start
  7.2 0.7 all-gather.3.cloned.1.call-update
  7.9 0.7 slice.94
  8.6 55.5 %all-gather = f32[1,2,512,128]{3,2,1,0:T(8,128)S(1)} all-gather(f32[1,2,16,128]{3,2,1,0:T(8,128)S(1)} %slice.94), channel_id=2, replica_groups=mesh['row'=32,'col'=16] {'row'}, dimensions={2}, use_global_device_ids=true | all-gather | bytes 540672 | tf_op jit(solution)/shard_map/all_gather | solution.py:24
  64.2 1.0 fusion.26
  65.2 1.0 fusion.15
  66.2 1.0 fusion.27
  67.2 1.0 fusion.14
  68.2 48.7 %all_gather.16 = f32[2,512,128]{2,1,0:T(8,128)S(1)} all-gather(f32[2,16,128]{2,1,0:T(8,128)S(1)} %get-tuple-element.8), channel_id=1, replica_groups=mesh['row'=32,'col'=16] {'row'}, dimensions={1}, use_global_device_ids=true | all-gather | bytes 540672 | tf_op jit(solution)/shard_map/all_gather | solution.py:25
  117.0 1.0 fusion.28
  118.0 1.0 fusion.13
  119.0 1.0 fusion.29
  120.0 1.0 fusion.12
  121.1 0.7 maximum_subtract_fusion.1
  121.8 47.0 %all_gather.17 = f32[2,512,128]{2,1,0:T(8,128)S(1)} all-gather(f32[2,16,128]{2,1,0:T(8,128)S(1)} %maximum_subtract_fusion.1), channel_id=1, replica_groups=mesh['row'=32,'col'=16] {'row'}, dimensions={1}, use_global_device_ids=true | all-gather | bytes 540672 | tf_op jit(solution)/shard_map/all_gather | solution.py:27
  168.8 1.0 fusion.30
  169.8 1.0 fusion.11
  170.9 1.0 fusion.31
  171.9 1.0 fusion.10
  172.9 48.7 %all_gather.18 = f32[2,512,128]{2,1,0:T(8,128)S(1)} all-gather(f32[2,16,128]{2,1,0:T(8,128)S(1)} %get-tuple-element.6), channel_id=1, replica_groups=mesh['row'=32,'col'=16] {'row'}, dimensions={1}, use_global_device_ids=true | all-gather | bytes 540672 | tf_op jit(solution)/shard_map/all_gather | solution.py:28
  221.7 0.0 copy-done.1
  221.7 1.0 fusion.20
  222.7 1.0 fusion.9
  223.7 1.0 fusion.18
  224.7 1.0 fusion.8
  225.8 0.8 copy.11
  226.5 0.0 copy-done.2
  226.5 0.3 copy.9
  226.9 0.6 pad_maximum_fusion.1
  227.5 0.0 all-gather.3.cloned.1.call-done
  227.5 0.0 copy-start
  227.5 4.7 %fusion.1 = f32[128,1024]{1,0:T(8,128)S(1)} fusion(f32[2,1024,1024]{1,2,0:T(8,128)} %all-gather.3.cloned.1.call-done, f32[2,1024,128]{2,1,0:T(8,128)S(1)} %constant_dynamic-update-slice_fusion), kind=kOutput, calls=%fused_computation.3 | convolution fusion | flops 1610612736 | bytes 5242880 | tf_op jit(solution)/shard_map/dot_general | solution.py:8
  232.2 4.6 %fusion = f32[128,1024]{1,0:T(8,128)S(1)} fusion(f32[2,1024,1024]{1,2,0:T(8,128)} %all-gather.3.cloned.1.call-done, f32[2,1024,128]{2,1,0:T(8,128)S(1)} %constant_dynamic-update-slice_fusion), kind=kOutput, calls=%fused_computation.2 | convolution fusion | flops 1610612736 | bytes 5242880 | tf_op jit(solution)/shard_map/dot_general | solution.py:8
  236.8 0.0 copy-done
  236.8 2.7 %fusion.7 = f32[1,1024,128]{1,2,0:T(8,128)S(1)} fusion(f32[128,1024]{1,0:T(8,128)S(1)} %fusion.1, f32[2,1024,1024]{1,2,0:T(8,128)S(1)} %copy-done, f32[2,1024,128]{2,1,0:T(8,128)S(1)} %constant_dynamic-update-slice_fusion), kind=kOutput, calls=%fused_computation.9 | convolution fusion | flops 1610743808 | bytes 5767168 | tf_op jit(solution)/shard_map/dot_general | solution.py:8
  239.5 2.4 fusion.6
  241.9 0.2 maximum_subtract_fusion
  242.1 1.3 copy.10
  (5 shorter events, 0.1 us)
Async XLA Ops:
  7.2 214.6 %copy-start.1 = (f32[2,128,1024]{2,1,0:T(8,128)S(1)}, f32[2,128,1024]{2,1,0:T(8,128)}, u32[]{:S(2)}) copy-start(f32[2,128,1024]{2,1,0:T(8,128)} %param.11) | copy-start | bytes 3145732
  7.2 219.3 %copy-start.2 = (f32[2,1024,128]{2,1,0:T(8,128)S(1)}, f32[2,1024,128]{2,1,0:T(8,128)}, u32[]{:S(2)}) copy-start(f32[2,1024,128]{2,1,0:T(8,128)} %param.6) | copy-start | bytes 3145732
  7.2 220.3 %all-gather.3.cloned.1.call-start = ((), (), s32[]{:S(2)}) async-start(), calls=%async_computation | async-start | bytes 8912896 | tf_op jit(solution)/shard_map/all_gather | solution.py:31
  227.5 9.3 %copy-start = (f32[2,1024,1024]{1,2,0:T(8,128)S(1)}, f32[2,1024,1024]{1,2,0:T(8,128)}, u32[]{:S(2)}) copy-start(f32[2,1024,1024]{1,2,0:T(8,128)} %all-gather.3.cloned.1.call-done) | copy-start | bytes 25165828
Sparse Core Ops, SparseCore 0:
  10.1 60.7 all-gather.2
where the time goes:
time: 251 us; the launch traced here: 250 us
  blocking collectives  200 us (80%)
  matrix products  30.5 us (12%)
  between operations  14.3 us (6%)
  local copies, waits for them, and re-layouts  3.2 us (1%)
    all_gather x1, blocking collectives, local(): lax.all_gather(rhs_low[1], 'row', axis=1, tiled=True)  55.5 us
    all_gather x1, blocking collectives, local(): lower_all = lax.all_gather(lower_part, 'row', axis=1, tiled=True)  48.7 us
    all_gather x1, blocking collectives, local(): upper_all = lax.all_gather(upper_part, 'row', axis=1, tiled=True)  48.7 us
    all_gather x1, blocking collectives, local(): lax.all_gather(reduced, 'row', axis=1, tiled=True)  47 us
    dot_general x20, matrix products, plain_product(): jnp.dot(left_side, right_side, precision=lax.Precision.HIGHEST, preferred...  30.5 us
  transfers between devices with their start and end apart: 1, of which 0 were waited for; matrix products, arithmetic and copies ran while one was open for 8% of the time, Pallas kernels for 0%

commit v1 on v0

v1 whole, which is shorter than its diff:
```python
import jax
import jax.numpy as jnp
from jax import lax
from jax.sharding import PartitionSpec as P


def product(left_side, right_side):
    return jnp.dot(left_side, right_side, precision=lax.Precision.HIGH, preferred_element_type=jnp.float32)


def rows_of(matrix):
    return matrix.reshape(matrix.shape[0] * matrix.shape[1], matrix.shape[2])


def joined(pair):
    return jnp.concatenate([pair[0], pair[1]], axis=1)


def combine(four):
    m, n = four.shape[0] // 2, four.shape[1] // 2
    real_part = four[:m, :n] - four[m:, n:]
    imag_part = four[:m, n:] + four[m:, :n]
    return jnp.concatenate([real_part, imag_part], axis=1)


def split(wide):
    n = wide.shape[1] // 2
    return jnp.stack([wide[:, :n], wide[:, n:]], axis=0)


def everyone(piece):
    count = lax.axis_size("row")
    spread = jnp.broadcast_to(piece[None], (count,) + piece.shape)
    return lax.all_to_all(spread, "row", 0, 0, tiled=True).reshape(count * piece.shape[0], piece.shape[1])


def tall_product(left_side, right_side):
    return lax.dot_general(left_side, right_side, (((0,), (0,)), ((), ())), precision=lax.Precision.HIGH, preferred_element_type=jnp.float32)


def local(rhs_top, rhs_low, inv_diag, coupling, panel, radiation):
    half = coupling.shape[2]
    wide_panel = lax.all_gather(jnp.swapaxes(panel, 1, 2), "col", axis=1, tiled=True)
    last_all = everyone(joined(rhs_low[1]))
    lower = combine(product(rows_of(inv_diag[1]), last_all))
    lower_all = everyone(lower)
    reduced = joined(rhs_low[0]) - combine(product(rows_of(coupling), lower_all))
    reduced_all = everyone(reduced)
    upper = combine(product(rows_of(inv_diag[0]), reduced_all))
    upper_all = everyone(upper)
    currents = jnp.concatenate([upper_all, lower_all], axis=0)
    far_field = split(combine(product(rows_of(radiation), currents)))
    real_rows = tall_product(wide_panel[0], currents)
    imag_rows = tall_product(wide_panel[1], currents)
    n = rhs_top.shape[2]
    updated_top = jnp.stack([
        rhs_top[0] - (real_rows[:, :n] - imag_rows[:, n:]),
        rhs_top[1] - (real_rows[:, n:] + imag_rows[:, :n]),
    ], axis=0)
    solved = jnp.stack([split(upper), split(lower)], axis=0)
    return (solved, updated_top, far_field)


def solution(mesh):
    in_specs = (
        P(None, "row", "col"),
        P(None, None, "row", "col"),
        P(None, None, "row", None),
        P(None, "row", None),
        P(None, "row", "col"),
        P(None, "row", None),
    )
    out_specs = (P(None, None, "row", "col"), P(None, "row", "col"), P(None, "row", "col"))
    return jax.shard_map(local, mesh=mesh, in_specs=in_specs, out_specs=out_specs, check_vma=False)
```

time: 251 us -> 127 us (0.51)
  blocking collectives: 200 us -> 43.6 us
  waiting for transfers between devices: 0.68 us -> 29 us
  matrix products: 30.5 us -> 10.8 us
  starting transfers between devices: 0.04 us -> 18.4 us
  local copies, waits for them, and re-layouts: 3.2 us -> 8.85 us
    all_gather x4 -> x0, blocking collectives: 200 us -> none  [the longest x1 55.5 us: local(): lax.all_gather(rhs_low[1], 'row', axis=1, tiled=True)]
    all_to_all x0 -> x2, blocking collectives: none -> 43.6 us  [everyone(): lax.all_to_all(spread, 'row', 0, 0, tiled=True)]
    all_to_all x0 -> x2, waiting for transfers between devices: none -> 28.3 us  [everyone(): lax.all_to_all(spread, 'row', 0, 0, tiled=True)]
    dot_general x20 -> x6, matrix products: 30.5 us -> 10.8 us  [the longest x2 8.24 us: tall_product(): lax.dot_general(left_side, right_side, (((0,), (0,)), ((), ())), precisio...]
    all_to_all x0 -> x2, starting transfers between devices: none -> 18.4 us  [everyone(): lax.all_to_all(spread, 'row', 0, 0, tiled=True)]
  transfers between devices with their start and end apart: 1 -> 3, of which waited for: 0 -> 2; matrix products, arithmetic and copies ran while one was open for 8% -> 9% of each run, Pallas kernels for 0% -> 0%
where the time goes in v1:
time: 127 us; the launch traced here: 126 us
  blocking collectives  43.6 us (34%)
  waiting for transfers between devices  29 us (23%)
  starting transfers between devices  18.4 us (14%)
  between operations  14.2 us (11%)
  matrix products  10.8 us (9%)
  local copies, waits for them, and re-layouts  8.85 us (7%)
    all_to_all x2, blocking collectives, everyone(): lax.all_to_all(spread, 'row', 0, 0, tiled=True)  43.6 us
    all_to_all x2, waiting for transfers between devices, everyone(): lax.all_to_all(spread, 'row', 0, 0, tiled=True)  28.3 us
    all_to_all x2, starting transfers between devices, everyone(): lax.all_to_all(spread, 'row', 0, 0, tiled=True)  18.4 us
    dot_general x2, matrix products, tall_product(): lax.dot_general(left_side, right_side, (((0,), (0,)), ((), ())), precisio...  8.24 us
    unnamed x10, local copies, waits for them, and re-layouts  4.14 us
    dot_general x4, matrix products, product(): jnp.dot(left_side, right_side, precision=lax.Precision.HIGH, preferred_el...  2.61 us
  transfers between devices with their start and end apart: 3, of which 2 were waited for; matrix products, arithmetic and copies ran while one was open for 9% of the time, Pallas kernels for 0%

profile of v1, /device:TPU:56, one launch (start us, length us, event | category | flops | bytes accessed | tf_op | source)
XLA Modules:
  0.0 126.0 jit_solution(2280643016953884918)
XLA Ops:
  7.2 0.0 copy-start
  7.2 0.0 all-gather.2.cloned.1.call-start
  7.2 0.7 all-gather.2.cloned.1.call-update
  7.9 0.8 slice_bitcast_fusion.11
  8.7 0.9 broadcast_in_dim.8
  9.5 13.2 %all-to-all-start = ((f32[32,16,256]{2,1,0:T(8,128)}), f32[32,16,256]{2,1,0:T(8,128)S(1)}, u32[]{:S(2)}, u32[]{:S(2)}) async-start(f32[32,16,256]{2,1,0:T(8,128)} %broadcast_in_dim.8), calls=%async_computation | async-start | bytes 1048576 | tf_op jit(solution)/shard_map/all_to_all | solution.py:34
  22.7 0.9 fusion.14
  23.6 15.8 %all-to-all-done = f32[32,16,256]{2,1,0:T(8,128)S(1)} async-done(((f32[32,16,256]{2,1,0:T(8,128)}), f32[32,16,256]{2,1,0:T(8,128)S(1)}, u32[]{:S(2)}, u32[]{:S(2)}) %all-to-all-start) | async-done | bytes 524320 | tf_op jit(solution)/shard_map/all_to_all | solution.py:34
  39.4 0.3 convolution_bitcast_fusion.3
  39.7 0.1 broadcast_in_dim.9
  39.8 22.1 %all_to_all.20 = f32[32,16,256]{2,1,0:T(8,128)S(1)} all-to-all(f32[32,16,256]{2,1,0:T(8,128)S(1)} %broadcast_in_dim.9), channel_id=1, replica_groups=mesh['row'=32,'col'=16] {'row'}, dimensions={0} | all-to-all | bytes 1048576 | tf_op jit(solution)/shard_map/all_to_all | solution.py:34
  61.8 1.1 convolution_bitcast_fusion.2
  63.0 0.1 broadcast_in_dim.10
  63.0 21.6 %all_to_all.21 = f32[32,16,256]{2,1,0:T(8,128)S(1)} all-to-all(f32[32,16,256]{2,1,0:T(8,128)S(1)} %broadcast_in_dim.10), channel_id=1, replica_groups=mesh['row'=32,'col'=16] {'row'}, dimensions={0} | all-to-all | bytes 1048576 | tf_op jit(solution)/shard_map/all_to_all | solution.py:34
  84.6 0.3 convolution_bitcast_fusion.1
  84.9 0.9 broadcast_in_dim.11
  85.7 5.2 %all-to-all-start.3 = ((f32[32,16,256]{2,1,0:T(8,128)}), f32[32,16,256]{2,1,0:T(8,128)S(1)}, u32[]{:S(2)}, u32[]{:S(2)}) async-start(f32[32,16,256]{2,1,0:T(8,128)} %broadcast_in_dim.11), calls=%async_computation.3 | async-start | bytes 1048576 | tf_op jit(solution)/shard_map/all_to_all | solution.py:34
  90.9 1.3 %fusion.13 = (f32[1,1024,128]{2,1,0:T(8,128)S(1)}, f32[1,1024,128]{2,1,0:T(8,128)S(1)}) fusion(f32[2,1024,128]{2,1,0:T(8,128)} %param.6), kind=kLoop, calls=%fused_computation.43 | loop fusion | bytes 2097152 | tf_op jit(solution)/shard_map/slice | solution.py:57
  92.2 1.0 copy.13
  93.3 0.0 copy-start.1
  93.3 1.0 copy.14
  94.3 0.0 copy-start.2
  94.3 0.6 pad_maximum_fusion.6
  94.9 12.5 %all-to-all-done.3 = f32[32,16,256]{2,1,0:T(8,128)S(1)} async-done(((f32[32,16,256]{2,1,0:T(8,128)}), f32[32,16,256]{2,1,0:T(8,128)S(1)}, u32[]{:S(2)}, u32[]{:S(2)}) %all-to-all-start.3) | async-done | bytes 524320 | tf_op jit(solution)/shard_map/all_to_all | solution.py:34
  107.4 0.0 copy-done
  107.4 1.0 convolution_bitcast_fusion
  108.4 0.8 copy.12
  109.2 0.0 all-gather.2.cloned.1.call-done
  109.2 4.1 %fusion.2 = f32[1024,256]{0,1:T(8,128)S(1)} fusion(f32[2,1024,1024]{2,1,0:T(8,128)} %all-gather.2.cloned.1.call-done, f32[512,256]{1,0:T(8,128)S(1)} %bitcast.69, f32[512,256]{1,0:T(8,128)S(1)} %bitcast.72), kind=kOutput, calls=%fused_computation.4 | convolution fusion | flops 1610874880 | bytes 6291456 | tf_op jit(solution)/shard_map/dot_general | solution.py:38
  113.3 4.1 %fusion.3 = f32[1024,256]{0,1:T(8,128)S(1)} fusion(f32[2,1024,1024]{2,1,0:T(8,128)} %all-gather.2.cloned.1.call-done, f32[512,256]{1,0:T(8,128)S(1)} %bitcast.70, f32[512,256]{1,0:T(8,128)S(1)} %bitcast.73), kind=kOutput, calls=%fused_computation.5 | convolution fusion | flops 1610874880 | bytes 6291456 | tf_op jit(solution)/shard_map/dot_general | solution.py:38
  117.5 0.0 copy-done.1
  117.5 0.0 copy-done.2
  117.5 0.3 fusion.7
  117.8 0.1 pad_maximum_fusion.1
  117.9 1.3 %copy.11 = f32[2,1024,128]{2,1,0:T(8,128)} copy(f32[2,1024,128]{1,2,0:T(8,128)S(1)} %pad_maximum_fusion.1) | data formatting | bytes 2097152
  (11 shorter events, 0.1 us)
Async XLA Ops:
  7.2 100.2 %copy-start = (f32[2,128,1024]{2,1,0:T(8,128)S(1)}, f32[2,128,1024]{2,1,0:T(8,128)}, u32[]{:S(2)}) copy-start(f32[2,128,1024]{2,1,0:T(8,128)} %param.11) | copy-start | bytes 3145732
  7.2 102.0 %all-gather.2.cloned.1.call-start = ((), (), s32[]{:S(2)}) async-start(), calls=%async_computation.4 | async-start | bytes 8912896 | tf_op jit(solution)/shard_map/all_gather | solution.py:43
  9.5 29.9 %all-to-all-start = ((f32[32,16,256]{2,1,0:T(8,128)}), f32[32,16,256]{2,1,0:T(8,128)S(1)}, u32[]{:S(2)}, u32[]{:S(2)}) async-start(f32[32,16,256]{2,1,0:T(8,128)} %broadcast_in_dim.8), calls=%async_computation | async-start | bytes 1048576 | tf_op jit(solution)/shard_map/all_to_all | solution.py:34
  85.7 21.7 %all-to-all-start.3 = ((f32[32,16,256]{2,1,0:T(8,128)}), f32[32,16,256]{2,1,0:T(8,128)S(1)}, u32[]{:S(2)}, u32[]{:S(2)}) async-start(f32[32,16,256]{2,1,0:T(8,128)} %broadcast_in_dim.11), calls=%async_computation.3 | async-start | bytes 1048576 | tf_op jit(solution)/shard_map/all_to_all | solution.py:34
  93.3 24.2 %copy-start.1 = (f32[1,1024,128]{1,2,0:T(8,128)S(1)}, f32[1,1024,128]{1,2,0:T(8,128)}, u32[]{:S(2)}) copy-start(f32[1,1024,128]{1,2,0:T(8,128)} %copy.13) | copy-start | bytes 1572868
  94.3 23.2 %copy-start.2 = (f32[1,1024,128]{1,2,0:T(8,128)S(1)}, f32[1,1024,128]{1,2,0:T(8,128)}, u32[]{:S(2)}) copy-start(f32[1,1024,128]{1,2,0:T(8,128)} %copy.14) | copy-start | bytes 1572868
Sparse Core Ops, SparseCore 0:
  10.1 60.7 all-gather.1

commit v2 on v0

v2 whole, which is shorter than its diff:
```python
import jax
import jax.numpy as jnp
from jax import lax
from jax.experimental import pallas as pl
from jax.experimental.pallas import tpu as pltpu
from jax.sharding import Mesh, PartitionSpec as P

XS, ZS = 4, 8


def product(left_side, right_side):
    return jnp.dot(left_side, right_side, precision=lax.Precision.HIGH, preferred_element_type=jnp.float32)


def exchange(pieces, axes):
    return lax.all_to_all(pieces, axes, 0, 0, tiled=True)


def everyone(piece, axis):
    count = lax.axis_size(axis)
    return exchange(jnp.broadcast_to(piece[None], (count,) + piece.shape), axis)


def complex_rows(matrix, vector):
    x, _, r, k = matrix.shape
    n = vector.shape[1]
    four = product(matrix.reshape(x * 2 * r, k), vector).reshape(x, 2, r, n)
    by_real, by_imag = four[:, 0], four[:, 1]
    turned = jnp.concatenate([-by_imag[..., n // 2:], by_imag[..., : n // 2]], axis=-1)
    return by_real + turned


def along_z(piece, before, after):
    padded = jnp.pad(piece, ((0, 0), (0, 0), (before, after)))
    got = everyone(padded, "z")
    x, r, n = padded.shape
    return jnp.swapaxes(got, 0, 1).reshape(x * ZS * r, n)


def halves(value):
    high = value.astype(jnp.bfloat16)
    return high, (value - high.astype(jnp.float32)).astype(jnp.bfloat16)


def dot_three(stacked, right_side, contract):
    m = stacked.shape[0] // 2
    high, low = halves(right_side)
    dims = (((1,), (contract,)), ((), ()))
    both = lax.dot_general(stacked, high, dims, preferred_element_type=jnp.float32)
    rest = lax.dot_general(stacked[:m], low, dims, preferred_element_type=jnp.float32)
    return both[:m] + both[m:] + rest


def parts_of(by_real, by_imag):
    n = by_real.shape[0] // 2
    return (by_real[:n] - by_imag[n:]).T, (by_real[n:] + by_imag[:n]).T


def spread(place_ref, upper_ref, lower_ref, radiation_ref, turned_ref, far_ref, solved_ref):
    s, zs, _, lanes = upper_ref.shape
    a = lanes // 4
    n = s * a
    r = solved_ref.shape[2]
    half = lower_ref.shape[1]
    x, z = place_ref[0], place_ref[1]
    right_half = x >= 2
    inner = x - 2 * right_half.astype(jnp.int32)
    upper_at = pl.multiple_of(inner * r, r)
    lower_at = pl.multiple_of((inner * zs + z) * r, r)
    mine = (
        [upper_ref[i, z, pl.ds(upper_at, r), :] for i in range(s)],
        [lower_ref[i, pl.ds(lower_at, r), :] for i in range(s)],
    )
    for block in range(2):
        pieces = [jnp.where(right_half, piece[:, 2 * a:], piece[:, :2 * a]) for piece in mine[block]]
        for part in range(2):
            solved_ref[block, part] = jnp.concatenate([piece[:, part * a:(part + 1) * a] for piece in pieces], axis=1)
    for i in range(s):
        ordered = jnp.concatenate([upper_ref[i, k, j * r:(j + 1) * r, :] for j in range(2) for k in range(zs)], axis=0)
        for block, value in enumerate((ordered, lower_ref[i])):
            high, low = halves(value.T)
            for h in range(2):
                for part in range(2):
                    at = (h * 2 + part) * a
                    to = part * n + i * a
                    k = (block * 2 + h) * half
                    turned_ref[to:to + a, k:k + half] = high[at:at + a]
                    turned_ref[2 * n + to:2 * n + to + a, k:k + half] = low[at:at + a]
    turned = turned_ref[...]
    real_part, imag_part = parts_of(dot_three(turned, radiation_ref[0], 1), dot_three(turned, radiation_ref[1], 1))
    far_ref[0] = real_part
    far_ref[1] = imag_part


def finish_kernel(place_ref, upper_ref, lower_ref, radiation_ref, panel_ref, top_ref, far_ref, solved_ref, out_ref, turned_ref):
    @pl.when(pl.program_id(0) == 0)
    def _():
        spread(place_ref, upper_ref, lower_ref, radiation_ref, turned_ref, far_ref, solved_ref)

    turned = turned_ref[...]
    real_part, imag_part = parts_of(dot_three(turned, panel_ref[0], 0), dot_three(turned, panel_ref[1], 0))
    out_ref[0] = top_ref[0] - real_part
    out_ref[1] = top_ref[1] - imag_part


def finish(place, upper, lower, radiation, wide_panel, rhs_top, r, tile=256):
    _, k, m = wide_panel.shape
    n = rhs_top.shape[2]

    def whole(shape):
        return pl.BlockSpec(shape, lambda i: (0,) * len(shape))

    far, solved = (2, radiation.shape[1], n), (2, 2, r, n)
    return pl.pallas_call(
        finish_kernel,
        out_shape=tuple(jax.ShapeDtypeStruct(shape, jnp.float32) for shape in (far, solved, rhs_top.shape)),
        grid=(m // tile,),
        in_specs=[
            pl.BlockSpec(memory_space=pltpu.SMEM),
            whole(upper.shape),
            whole(lower.shape),
            whole(radiation.shape),
            pl.BlockSpec((2, k, tile), lambda i: (0, 0, i)),
            pl.BlockSpec((2, tile, n), lambda i: (0, i, 0)),
        ],
        out_specs=(whole(far), whole(solved), pl.BlockSpec((2, tile, n), lambda i: (0, i, 0))),
        scratch_shapes=[pltpu.VMEM((4 * n, k), jnp.bfloat16)],
        compiler_params=pltpu.CompilerParams(vmem_limit_bytes=48 * 1024 * 1024),
        name="finish",
    )(place, upper, lower, radiation, wide_panel, rhs_top)


def local(rhs_top, rhs_low, inv_diag, coupling, panel, radiation):
    r, n = rhs_low.shape[2], rhs_low.shape[3]
    half = coupling.shape[2]
    a = n // XS
    matrices = lax.all_gather(jnp.stack([inv_diag[1], coupling, inv_diag[0]], axis=0), "x", axis=0)
    wide_panel = lax.all_gather(jnp.swapaxes(panel, 1, 2), "col", axis=1, tiled=True)
    quarters = jnp.stack([
        jnp.concatenate([rhs_low[block, part, :, i * a:(i + 1) * a] for block in range(2) for part in range(2)], axis=1)
        for i in range(XS)], axis=0)[:, None]
    quarters = jnp.broadcast_to(quarters, (XS, ZS, r, 4 * a)).reshape(XS * ZS, r, 4 * a)
    right = exchange(quarters, ("x", "z"))
    first = lax.dynamic_index_in_dim(right.reshape(XS, ZS, r, 4 * a), lax.axis_index("z"), 1, keepdims=False)
    first, right = lax.optimization_barrier((first, right.reshape(half, 4 * a)))
    lower_all = along_z(complex_rows(matrices[:, 0], right[:, 2 * a:]), 2 * a, 0)
    reduced = first[:, :, :2 * a] - complex_rows(matrices[:, 1], lower_all[:, 2 * a:])
    reduced_all = along_z(reduced, 0, 2 * a)
    upper = complex_rows(matrices[:, 2], reduced_all[:, :2 * a])
    upper, lower_all = lax.optimization_barrier((upper, lower_all))
    lower_pack = jnp.concatenate([lower_all[:half // 2, 2 * a:], lower_all[half // 2:, 2 * a:]], axis=1)
    upper_pack = jnp.concatenate([upper[:XS // 2], upper[XS // 2:]], axis=2).reshape(1, XS // 2 * r, 4 * a)
    upper_all = exchange(jnp.broadcast_to(upper_pack, (XS * ZS,) + upper_pack.shape[1:]), ("x", "z"))
    lower_wide = lax.all_gather(lower_pack, "x", axis=0)
    place = jnp.stack([lax.axis_index("x"), lax.axis_index("z")]).astype(jnp.int32)
    upper_all = upper_all.reshape((XS, ZS) + upper_pack.shape[1:])
    far_field, solved, updated_top = finish(place, upper_all, lower_wide, radiation, wide_panel, rhs_top, r)
    return (solved, updated_top, far_field)


def solution(mesh):
    fine = Mesh(mesh.devices.reshape(XS, ZS, -1), ("x", "z", "col"))
    row = ("x", "z")
    in_specs = (
        P(None, row, "col"),
        P(None, None, row, "col"),
        P(None, None, row, None),
        P(None, row, None),
        P(None, row, "col"),
        P(None, row, None),
    )
    out_specs = (P(None, None, row, "col"), P(None, row, "col"), P(None, row, "col"))
    return jax.shard_map(local, mesh=fine, in_specs=in_specs, out_specs=out_specs, check_vma=False)
```

time: 251 us -> 108 us (0.43)
  blocking collectives: 200 us -> 59.4 us
  matrix products: 30.5 us -> 0.89 us
  starting transfers between devices: 0.04 us -> 18 us
  Pallas kernels: 0 us -> 8.7 us
    all_gather x4 -> x2, blocking collectives: 200 us -> 30.2 us  [the longest x1 15.2 us: local(): lower_wide = lax.all_gather(lower_pack, 'x', axis=0)]
    dot_general x20 -> x3, matrix products: 30.5 us -> 0.89 us  [product(): jnp.dot(left_side, right_side, precision=lax.Precision.HIGH, preferred_el...]
    all_to_all x0 -> x2, blocking collectives: none -> 29.2 us  [exchange(): return lax.all_to_all(pieces, axes, 0, 0, tiled=True)]
    all_to_all x0 -> x2, starting transfers between devices: none -> 17.9 us  [exchange(): return lax.all_to_all(pieces, axes, 0, 0, tiled=True)]
    pallas_call x0 -> x1, Pallas kernels: none -> 8.7 us  [finish(): pl.pallas_call(finish_kernel, out_shape=tuple((jax.ShapeDtypeStruct(shape...]
  transfers between devices with their start and end apart: 1 -> 3, of which waited for: 0 -> 0; matrix products, arithmetic and copies ran while one was open for 8% -> 6% of each run, Pallas kernels for 0% -> 0%
where the time goes in v2:
time: 108 us; the launch traced here: 107 us
  blocking collectives  59.4 us (55%)
  starting transfers between devices  18 us (17%)
  between operations  14.2 us (13%)
  Pallas kernels  8.7 us (8%)
  local copies, waits for them, and re-layouts  3.91 us (4%)
  other arithmetic  1.74 us (2%)
    all_to_all x2, blocking collectives, exchange(): return lax.all_to_all(pieces, axes, 0, 0, tiled=True)  29.2 us
    all_to_all x2, starting transfers between devices, exchange(): return lax.all_to_all(pieces, axes, 0, 0, tiled=True)  17.9 us
    all_gather x1, blocking collectives, local(): lower_wide = lax.all_gather(lower_pack, 'x', axis=0)  15.2 us
    all_gather x1, blocking collectives, local(): lax.all_gather(jnp.stack([inv_diag[1], coupling, inv_diag[0]], axis=0), '...  15 us
    pallas_call x1, Pallas kernels, finish(): pl.pallas_call(finish_kernel, out_shape=tuple((jax.ShapeDtypeStruct(shape...  8.7 us
  transfers between devices with their start and end apart: 3, of which 0 were waited for; matrix products, arithmetic and copies ran while one was open for 6% of the time, Pallas kernels for 0%

profile of v2, /device:TPU:56, one launch (start us, length us, event | category | flops | bytes accessed | tf_op | source)
XLA Modules:
  0.0 107.5 jit_solution(8584508503206901301)
XLA Ops:
  7.2 0.0 copy-start
  7.2 0.0 copy-start.1
  7.2 0.0 all-gather.4.cloned.1.call-start
  7.2 0.7 all-gather.4.cloned.1.call-update
  7.9 1.0 slice_bitcast_fusion.33
  8.9 0.1 maximum_bitcast_fusion
  9.0 0.1 maximum_bitcast_fusion.2
  9.1 0.7 broadcast_in_dim.10
  9.8 13.2 %all-to-all-start = ((f32[32,16,128]{2,1,0:T(8,128)}), f32[32,16,128]{2,1,0:T(8,128)S(1)}, u32[]{:S(2)}, u32[]{:S(2)}) async-start(f32[32,16,128]{2,1,0:T(8,128)} %bitcast.25), calls=%async_computation | async-start | bytes 524288 | tf_op jit(solution)/shard_map/all_to_all | solution.py:16
  23.0 0.9 fusion.8
  23.9 0.9 pad_maximum_fusion
  24.7 15.0 %all-gather = f32[12,2,16,512]{3,2,1,0:T(8,128)S(1)} all-gather(f32[3,2,16,512]{3,2,1,0:T(8,128)S(1)} %pad_maximum_fusion), channel_id=2, replica_groups=mesh['x'=4,'z'=8,'col'=16] {'x'}, dimensions={0}, use_global_device_ids=true | all-gather | bytes 983040 | tf_op jit(solution)/shard_map/all_gather | solution.py:137
  39.7 0.0 all-to-all-done
  39.7 0.1 copy.31
  39.9 0.3 fusion.2
  40.1 0.1 slice_negate_fusion.2
  40.2 0.1 fusion.6
  40.3 0.1 pad.8
  40.4 16.3 %all_to_all.20 = f32[8,4,16,128]{3,2,1,0:T(8,128)S(1)} all-to-all(f32[8,4,16,128]{3,2,1,0:T(8,128)S(1)} %broadcast_in_dim.11), channel_id=1, replica_groups=mesh['x'=4,'z'=8,'col'=16] {'z'}, dimensions={0} | all-to-all | bytes 524288 | tf_op jit(solution)/shard_map/all_to_all | solution.py:16
  56.8 0.4 fusion.1
  57.2 0.1 slice_negate_fusion.1
  57.2 0.1 fusion.5
  57.4 12.9 %all_to_all.21 = f32[8,4,16,128]{3,2,1,0:T(8,128)S(1)} all-to-all(f32[8,4,16,128]{3,2,1,0:T(8,128)S(1)} %broadcast_in_dim.12), channel_id=1, replica_groups=mesh['x'=4,'z'=8,'col'=16] {'z'}, dimensions={0} | all-to-all | bytes 524288 | tf_op jit(solution)/shard_map/all_to_all | solution.py:16
  70.3 0.3 fusion
  70.5 0.1 slice_negate_fusion
  70.6 0.1 fusion.3
  70.7 0.1 pad_maximum_fusion.3
  70.8 0.9 broadcast_in_dim.14
  71.7 4.8 %all-to-all-start.3 = ((f32[32,32,128]{2,1,0:T(8,128)}), f32[32,32,128]{2,1,0:T(8,128)S(1)}, u32[]{:S(2)}, u32[]{:S(2)}) async-start(f32[32,32,128]{2,1,0:T(8,128)} %broadcast_in_dim.14), calls=%async_computation.3 | async-start | bytes 1048576 | tf_op jit(solution)/shard_map/all_to_all | solution.py:16
  76.4 0.1 pad_add_fusion.place_ref
  76.5 0.1 fusion.7
  76.6 0.1 pad_maximum_fusion.1
  76.7 15.2 %all-gather.1 = f32[1024,128]{1,0:T(8,128)S(1)} all-gather(f32[256,128]{1,0:T(8,128)S(1)} %pad_maximum_fusion.1), channel_id=3, replica_groups=mesh['x'=4,'z'=8,'col'=16] {'x'}, dimensions={0}, use_global_device_ids=true | all-gather | bytes 655360 | tf_op jit(solution)/shard_map/all_gather | solution.py:154
  91.9 0.0 all-to-all-done.3
  91.9 0.0 all-gather.4.cloned.1.call-done.panel_ref
  91.9 0.0 copy-done
  91.9 0.0 copy-done.1
  91.9 8.7 %finish.1 = (f32[2,128,128]{2,1,0:T(8,128)}, f32[2,2,16,128]{3,2,1,0:T(8,128)}, f32[2,1024,128]{2,1,0:T(8,128)}) custom-call(s32[2]{0:T(128)S(1)} %pad_add_fusion.place_ref, f32[4,8,32,128]{3,2,1,0:T(8,128)S(1)} %bitcast.120, f32[4,256,128]{2,1,0:T(8,128)S(1)} %bitcast.119, f32[2,128,1024]{2,1,0:T(8,128)S(1)} %copy-done, ...), custom_call_target="tpu_custom_call" | custom-call | tf_op jit(solution)/shard_map/finish/pallas_call | solution.py:114
  (11 shorter events, 0.1 us)
Async XLA Ops:
  7.2 84.8 %copy-start = (f32[2,128,1024]{2,1,0:T(8,128)S(1)}, f32[2,128,1024]{2,1,0:T(8,128)}, u32[]{:S(2)}) copy-start(f32[2,128,1024]{2,1,0:T(8,128)} %radiation_ref.1) | copy-start | bytes 3145732
  7.2 84.7 %copy-start.1 = (f32[2,1024,128]{2,1,0:T(8,128)S(1)}, f32[2,1024,128]{2,1,0:T(8,128)}, u32[]{:S(2)}) copy-start(f32[2,1024,128]{2,1,0:T(8,128)} %top_ref.1) | copy-start | bytes 3145732
  7.2 84.7 %all-gather.4.cloned.1.call-start = ((), (), s32[]{:S(2)}) async-start(), calls=%async_computation.4 | async-start | bytes 8912896 | tf_op jit(solution)/shard_map/all_gather | solution.py:138
  9.8 29.9 %all-to-all-start = ((f32[32,16,128]{2,1,0:T(8,128)}), f32[32,16,128]{2,1,0:T(8,128)S(1)}, u32[]{:S(2)}, u32[]{:S(2)}) async-start(f32[32,16,128]{2,1,0:T(8,128)} %bitcast.25), calls=%async_computation | async-start | bytes 524288 | tf_op jit(solution)/shard_map/all_to_all | solution.py:16
  71.7 20.3 %all-to-all-start.3 = ((f32[32,32,128]{2,1,0:T(8,128)}), f32[32,32,128]{2,1,0:T(8,128)S(1)}, u32[]{:S(2)}, u32[]{:S(2)}) async-start(f32[32,32,128]{2,1,0:T(8,128)} %broadcast_in_dim.14), calls=%async_computation.3 | async-start | bytes 1048576 | tf_op jit(solution)/shard_map/all_to_all | solution.py:16
Sparse Core Ops, SparseCore 0:
  10.1 60.7 all-gather.3

commit v3 on v2

--- a/solution.py
+++ b/solution.py
@@ -103,7 +103,7 @@
     out_ref[1] = top_ref[1] - imag_part
 
 
-def finish(place, upper, lower, radiation, wide_panel, rhs_top, r, tile=256):
+def finish(place, upper, lower, radiation, wide_panel, rhs_top, r, tile=512):
     _, k, m = wide_panel.shape
     n = rhs_top.shape[2]
 
@@ -134,7 +134,7 @@
     r, n = rhs_low.shape[2], rhs_low.shape[3]
     half = coupling.shape[2]
     a = n // XS
-    matrices = lax.all_gather(jnp.stack([inv_diag[1], coupling, inv_diag[0]], axis=0), "x", axis=0)
+    matrices = lax.all_gather(jnp.concatenate([inv_diag, coupling[None]], axis=0), "x", axis=0)
     wide_panel = lax.all_gather(jnp.swapaxes(panel, 1, 2), "col", axis=1, tiled=True)
     quarters = jnp.stack([
         jnp.concatenate([rhs_low[block, part, :, i * a:(i + 1) * a] for block in range(2) for part in range(2)], axis=1)
@@ -143,10 +143,10 @@
     right = exchange(quarters, ("x", "z"))
     first = lax.dynamic_index_in_dim(right.reshape(XS, ZS, r, 4 * a), lax.axis_index("z"), 1, keepdims=False)
     first, right = lax.optimization_barrier((first, right.reshape(half, 4 * a)))
-    lower_all = along_z(complex_rows(matrices[:, 0], right[:, 2 * a:]), 2 * a, 0)
-    reduced = first[:, :, :2 * a] - complex_rows(matrices[:, 1], lower_all[:, 2 * a:])
+    lower_all = along_z(complex_rows(matrices[:, 1], right[:, 2 * a:]), 2 * a, 0)
+    reduced = first[:, :, :2 * a] - complex_rows(matrices[:, 2], lower_all[:, 2 * a:])
     reduced_all = along_z(reduced, 0, 2 * a)
-    upper = complex_rows(matrices[:, 2], reduced_all[:, :2 * a])
+    upper = complex_rows(matrices[:, 0], reduced_all[:, :2 * a])
     upper, lower_all = lax.optimization_barrier((upper, lower_all))
     lower_pack = jnp.concatenate([lower_all[:half // 2, 2 * a:], lower_all[half // 2:, 2 * a:]], axis=1)
     upper_pack = jnp.concatenate([upper[:XS // 2], upper[XS // 2:]], axis=2).reshape(1, XS // 2 * r, 4 * a)

time: 108 us -> 107 us (level)
  transfers between devices with their start and end apart: 3 -> 3, of which waited for: 0 -> 0; matrix products, arithmetic and copies ran while one was open for 6% -> 5% of each run, Pallas kernels for 0% -> 0%
where the time goes in v3:
time: 107 us; the launch traced here: 106 us
  blocking collectives  60.2 us (56%)
  starting transfers between devices  17.4 us (16%)
  between operations  14.2 us (13%)
  Pallas kernels  8.13 us (8%)
  local copies, waits for them, and re-layouts  3.03 us (3%)
  other arithmetic  1.85 us (2%)
    all_to_all x2, blocking collectives, exchange(): return lax.all_to_all(pieces, axes, 0, 0, tiled=True)  29 us
    all_to_all x2, starting transfers between devices, exchange(): return lax.all_to_all(pieces, axes, 0, 0, tiled=True)  17.4 us
    all_gather x1, blocking collectives, local(): lax.all_gather(jnp.concatenate([inv_diag, coupling[None]], axis=0), 'x',...  15.7 us
    all_gather x1, blocking collectives, local(): lower_wide = lax.all_gather(lower_pack, 'x', axis=0)  15.4 us
    pallas_call x1, Pallas kernels, finish(): pl.pallas_call(finish_kernel, out_shape=tuple((jax.ShapeDtypeStruct(shape...  8.13 us
  transfers between devices with their start and end apart: 3, of which 0 were waited for; matrix products, arithmetic and copies ran while one was open for 5% of the time, Pallas kernels for 0%

profile of v3, /device:TPU:56, one launch (start us, length us, event | category | flops | bytes accessed | tf_op | source)
XLA Modules:
  0.0 106.5 jit_solution(6005815515424552435)
XLA Ops:
  7.2 0.0 copy-start
  7.2 0.0 copy-start.1
  7.2 0.0 all-gather.4.cloned.1.call-start
  7.2 0.7 all-gather.4.cloned.1.call-update
  7.9 1.0 slice_bitcast_fusion.33
  8.9 0.1 maximum_bitcast_fusion
  9.0 0.1 maximum_bitcast_fusion.2
  9.1 0.7 broadcast_in_dim.13
  9.8 13.2 %all-to-all-start = ((f32[32,16,128]{2,1,0:T(8,128)}), f32[32,16,128]{2,1,0:T(8,128)S(1)}, u32[]{:S(2)}, u32[]{:S(2)}) async-start(f32[32,16,128]{2,1,0:T(8,128)} %bitcast.25), calls=%async_computation | async-start | bytes 524288 | tf_op jit(solution)/shard_map/all_to_all | solution.py:16
  23.0 1.0 pad_maximum_fusion
  24.0 15.7 %all-gather = f32[12,2,16,512]{3,2,1,0:T(8,128)S(1)} all-gather(f32[3,2,16,512]{3,2,1,0:T(8,128)S(1)} %pad_maximum_fusion), channel_id=2, replica_groups=mesh['x'=4,'z'=8,'col'=16] {'x'}, dimensions={0}, use_global_device_ids=true | all-gather | bytes 983040 | tf_op jit(solution)/shard_map/all_gather | solution.py:137
  39.7 0.0 all-to-all-done
  39.7 0.1 copy.31
  39.9 0.3 fusion.2
  40.1 0.1 slice_negate_fusion.2
  40.2 0.1 fusion.6
  40.3 0.1 pad.8
  40.4 16.2 %all_to_all.20 = f32[8,4,16,128]{3,2,1,0:T(8,128)S(1)} all-to-all(f32[8,4,16,128]{3,2,1,0:T(8,128)S(1)} %broadcast_in_dim.14), channel_id=1, replica_groups=mesh['x'=4,'z'=8,'col'=16] {'z'}, dimensions={0} | all-to-all | bytes 524288 | tf_op jit(solution)/shard_map/all_to_all | solution.py:16
  56.6 0.4 fusion.1
  57.0 0.1 slice_negate_fusion.1
  57.0 0.1 fusion.5
  57.2 12.9 %all_to_all.21 = f32[8,4,16,128]{3,2,1,0:T(8,128)S(1)} all-to-all(f32[8,4,16,128]{3,2,1,0:T(8,128)S(1)} %broadcast_in_dim.15), channel_id=1, replica_groups=mesh['x'=4,'z'=8,'col'=16] {'z'}, dimensions={0} | all-to-all | bytes 524288 | tf_op jit(solution)/shard_map/all_to_all | solution.py:16
  70.1 0.3 fusion
  70.4 0.1 slice_negate_fusion
  70.4 0.1 fusion.3
  70.5 0.1 pad_maximum_fusion.3
  70.6 0.9 broadcast_in_dim.33
  71.5 4.2 %all-to-all-start.3 = ((f32[32,32,128]{2,1,0:T(8,128)}), f32[32,32,128]{2,1,0:T(8,128)S(1)}, u32[]{:S(2)}, u32[]{:S(2)}) async-start(f32[32,32,128]{2,1,0:T(8,128)} %broadcast_in_dim.33), calls=%async_computation.3 | async-start | bytes 1048576 | tf_op jit(solution)/shard_map/all_to_all | solution.py:16
  75.7 0.1 pad_add_fusion.place_ref
  75.8 0.1 fusion.7
  75.9 0.1 pad_maximum_fusion.1
  76.0 15.4 %all-gather.1 = f32[1024,128]{1,0:T(8,128)S(1)} all-gather(f32[256,128]{1,0:T(8,128)S(1)} %pad_maximum_fusion.1), channel_id=3, replica_groups=mesh['x'=4,'z'=8,'col'=16] {'x'}, dimensions={0}, use_global_device_ids=true | all-gather | bytes 655360 | tf_op jit(solution)/shard_map/all_gather | solution.py:154
  91.5 0.0 all-to-all-done.3
  91.5 0.0 all-gather.4.cloned.1.call-done.panel_ref
  91.5 0.0 copy-done
  91.5 0.0 copy-done.1
  91.5 8.1 %finish.1 = (f32[2,128,128]{2,1,0:T(8,128)}, f32[2,2,16,128]{3,2,1,0:T(8,128)}, f32[2,1024,128]{2,1,0:T(8,128)}) custom-call(s32[2]{0:T(128)S(1)} %pad_add_fusion.place_ref, f32[4,8,32,128]{3,2,1,0:T(8,128)S(1)} %bitcast.120, f32[4,256,128]{2,1,0:T(8,128)S(1)} %bitcast.119, f32[2,128,1024]{2,1,0:T(8,128)S(1)} %copy-done, ...), custom_call_target="tpu_custom_call" | custom-call | tf_op jit(solution)/shard_map/finish/pallas_call | solution.py:114
  (11 shorter events, 0.1 us)
Async XLA Ops:
  7.2 84.3 %copy-start = (f32[2,128,1024]{2,1,0:T(8,128)S(1)}, f32[2,128,1024]{2,1,0:T(8,128)}, u32[]{:S(2)}) copy-start(f32[2,128,1024]{2,1,0:T(8,128)} %radiation_ref.1) | copy-start | bytes 3145732
  7.2 84.3 %copy-start.1 = (f32[2,1024,128]{2,1,0:T(8,128)S(1)}, f32[2,1024,128]{2,1,0:T(8,128)}, u32[]{:S(2)}) copy-start(f32[2,1024,128]{2,1,0:T(8,128)} %top_ref.1) | copy-start | bytes 3145732
  7.2 84.3 %all-gather.4.cloned.1.call-start = ((), (), s32[]{:S(2)}) async-start(), calls=%async_computation.4 | async-start | bytes 8912896 | tf_op jit(solution)/shard_map/all_gather | solution.py:138
  9.8 29.9 %all-to-all-start = ((f32[32,16,128]{2,1,0:T(8,128)}), f32[32,16,128]{2,1,0:T(8,128)S(1)}, u32[]{:S(2)}, u32[]{:S(2)}) async-start(f32[32,16,128]{2,1,0:T(8,128)} %bitcast.25), calls=%async_computation | async-start | bytes 524288 | tf_op jit(solution)/shard_map/all_to_all | solution.py:16
  71.5 20.0 %all-to-all-start.3 = ((f32[32,32,128]{2,1,0:T(8,128)}), f32[32,32,128]{2,1,0:T(8,128)S(1)}, u32[]{:S(2)}, u32[]{:S(2)}) async-start(f32[32,32,128]{2,1,0:T(8,128)} %broadcast_in_dim.33), calls=%async_computation.3 | async-start | bytes 1048576 | tf_op jit(solution)/shard_map/all_to_all | solution.py:16
Sparse Core Ops, SparseCore 0:
  10.1 60.7 all-gather.3

commit v4 on v3

--- a/solution.py
+++ b/solution.py
@@ -92,39 +92,39 @@
     far_ref[1] = imag_part
 
 
-def finish_kernel(place_ref, upper_ref, lower_ref, radiation_ref, panel_ref, top_ref, far_ref, solved_ref, out_ref, turned_ref):
-    @pl.when(pl.program_id(0) == 0)
-    def _():
-        spread(place_ref, upper_ref, lower_ref, radiation_ref, turned_ref, far_ref, solved_ref)
-
+def finish_kernel(place_ref, upper_ref, lower_ref, radiation_ref, panel_ref, top_ref, far_ref, solved_ref, out_ref, turned_ref, tiles_ref, arrived):
+    count, _, _, tile = tiles_ref.shape
+    copies = [
+        pltpu.make_async_copy(panel_ref.at[:, :, i * tile:(i + 1) * tile], tiles_ref.at[i], arrived.at[i])
+        for i in range(count)
+    ]
+    for copy in copies:
+        copy.start()
+    spread(place_ref, upper_ref, lower_ref, radiation_ref, turned_ref, far_ref, solved_ref)
     turned = turned_ref[...]
-    real_part, imag_part = parts_of(dot_three(turned, panel_ref[0], 0), dot_three(turned, panel_ref[1], 0))
-    out_ref[0] = top_ref[0] - real_part
-    out_ref[1] = top_ref[1] - imag_part
+    for i, copy in enumerate(copies):
+        copy.wait()
+        real_part, imag_part = parts_of(dot_three(turned, tiles_ref[i, 0], 0), dot_three(turned, tiles_ref[i, 1], 0))
+        rows = slice(i * tile, (i + 1) * tile)
+        out_ref[0, rows] = top_ref[0, rows] - real_part
+        out_ref[1, rows] = top_ref[1, rows] - imag_part
 
 
 def finish(place, upper, lower, radiation, wide_panel, rhs_top, r, tile=512):
     _, k, m = wide_panel.shape
     n = rhs_top.shape[2]
-
-    def whole(shape):
-        return pl.BlockSpec(shape, lambda i: (0,) * len(shape))
-
+    whole = pl.BlockSpec(memory_space=pltpu.VMEM)
     far, solved = (2, radiation.shape[1], n), (2, 2, r, n)
     return pl.pallas_call(
         finish_kernel,
         out_shape=tuple(jax.ShapeDtypeStruct(shape, jnp.float32) for shape in (far, solved, rhs_top.shape)),
-        grid=(m // tile,),
-        in_specs=[
-            pl.BlockSpec(memory_space=pltpu.SMEM),
-            whole(upper.shape),
-            whole(lower.shape),
-            whole(radiation.shape),
-            pl.BlockSpec((2, k, tile), lambda i: (0, 0, i)),
-            pl.BlockSpec((2, tile, n), lambda i: (0, i, 0)),
+        in_specs=[pl.BlockSpec(memory_space=pltpu.SMEM), whole, whole, whole, pl.BlockSpec(memory_space=pl.ANY), whole],
+        out_specs=(whole, whole, whole),
+        scratch_shapes=[
+            pltpu.VMEM((4 * n, k), jnp.bfloat16),
+            pltpu.VMEM((m // tile, 2, k, tile), jnp.float32),
+            pltpu.SemaphoreType.DMA((m // tile,)),
         ],
-        out_specs=(whole(far), whole(solved), pl.BlockSpec((2, tile, n), lambda i: (0, i, 0))),
-        scratch_shapes=[pltpu.VMEM((4 * n, k), jnp.bfloat16)],
         compiler_params=pltpu.CompilerParams(vmem_limit_bytes=48 * 1024 * 1024),
         name="finish",
     )(place, upper, lower, radiation, wide_panel, rhs_top)

time: 107 us -> 111 us (1.037)
  Pallas kernels: 8.13 us -> 11.6 us
    pallas_call x1, Pallas kernels: 8.13 us -> 11.6 us  [finish(): pl.pallas_call(finish_kernel, out_shape=tuple((jax.ShapeDtypeStruct(shape...]
where the time goes in v4:
time: 111 us; the launch traced here: 110 us
  blocking collectives  60.2 us (54%)
  starting transfers between devices  17.4 us (16%)
  between operations  14.2 us (13%)
  Pallas kernels  11.6 us (10%)
  local copies, waits for them, and re-layouts  3.03 us (3%)
  other arithmetic  1.85 us (2%)
    all_to_all x2, blocking collectives, exchange(): return lax.all_to_all(pieces, axes, 0, 0, tiled=True)  29 us
    all_to_all x2, starting transfers between devices, exchange(): return lax.all_to_all(pieces, axes, 0, 0, tiled=True)  17.4 us
    all_gather x1, blocking collectives, local(): lax.all_gather(jnp.concatenate([inv_diag, coupling[None]], axis=0), 'x',...  15.7 us
    all_gather x1, blocking collectives, local(): lower_wide = lax.all_gather(lower_pack, 'x', axis=0)  15.4 us
    pallas_call x1, Pallas kernels, finish(): pl.pallas_call(finish_kernel, out_shape=tuple((jax.ShapeDtypeStruct(shape...  11.6 us
  transfers between devices with their start and end apart: 3, of which 0 were waited for; matrix products, arithmetic and copies ran while one was open for 5% of the time, Pallas kernels for 0%

profile of v4, /device:TPU:56, one launch (start us, length us, event | category | flops | bytes accessed | tf_op | source)
XLA Modules:
  0.0 110.0 jit_solution(2013624209216494583)
XLA Ops:
  7.2 0.0 copy-start
  7.2 0.0 copy-start.1
  7.2 0.0 all-gather.4.cloned.1.call-start
  7.2 0.7 all-gather.4.cloned.1.call-update
  7.9 1.0 slice_bitcast_fusion.33
  8.9 0.1 maximum_bitcast_fusion
  9.0 0.1 maximum_bitcast_fusion.2
  9.1 0.7 broadcast_in_dim.13
  9.8 13.2 %all-to-all-start = ((f32[32,16,128]{2,1,0:T(8,128)}), f32[32,16,128]{2,1,0:T(8,128)S(1)}, u32[]{:S(2)}, u32[]{:S(2)}) async-start(f32[32,16,128]{2,1,0:T(8,128)} %bitcast.25), calls=%async_computation | async-start | bytes 524288 | tf_op jit(solution)/shard_map/all_to_all | solution.py:16
  23.0 1.0 pad_maximum_fusion
  24.0 15.7 %all-gather = f32[12,2,16,512]{3,2,1,0:T(8,128)S(1)} all-gather(f32[3,2,16,512]{3,2,1,0:T(8,128)S(1)} %pad_maximum_fusion), channel_id=2, replica_groups=mesh['x'=4,'z'=8,'col'=16] {'x'}, dimensions={0}, use_global_device_ids=true | all-gather | bytes 983040 | tf_op jit(solution)/shard_map/all_gather | solution.py:137
  39.7 0.0 all-to-all-done
  39.7 0.1 copy.31
  39.9 0.3 fusion.2
  40.1 0.1 slice_negate_fusion.2
  40.2 0.1 fusion.6
  40.3 0.1 pad.8
  40.4 16.2 %all_to_all.20 = f32[8,4,16,128]{3,2,1,0:T(8,128)S(1)} all-to-all(f32[8,4,16,128]{3,2,1,0:T(8,128)S(1)} %broadcast_in_dim.14), channel_id=1, replica_groups=mesh['x'=4,'z'=8,'col'=16] {'z'}, dimensions={0} | all-to-all | bytes 524288 | tf_op jit(solution)/shard_map/all_to_all | solution.py:16
  56.6 0.4 fusion.1
  57.0 0.1 slice_negate_fusion.1
  57.0 0.1 fusion.5
  57.2 12.9 %all_to_all.21 = f32[8,4,16,128]{3,2,1,0:T(8,128)S(1)} all-to-all(f32[8,4,16,128]{3,2,1,0:T(8,128)S(1)} %broadcast_in_dim.15), channel_id=1, replica_groups=mesh['x'=4,'z'=8,'col'=16] {'z'}, dimensions={0} | all-to-all | bytes 524288 | tf_op jit(solution)/shard_map/all_to_all | solution.py:16
  70.1 0.3 fusion
  70.4 0.1 slice_negate_fusion
  70.4 0.1 fusion.3
  70.5 0.1 pad_maximum_fusion.3
  70.6 0.9 broadcast_in_dim.33
  71.5 4.2 %all-to-all-start.3 = ((f32[32,32,128]{2,1,0:T(8,128)}), f32[32,32,128]{2,1,0:T(8,128)S(1)}, u32[]{:S(2)}, u32[]{:S(2)}) async-start(f32[32,32,128]{2,1,0:T(8,128)} %broadcast_in_dim.33), calls=%async_computation.3 | async-start | bytes 1048576 | tf_op jit(solution)/shard_map/all_to_all | solution.py:16
  75.7 0.1 pad_add_fusion.place_ref
  75.8 0.1 fusion.7
  75.9 0.1 pad_maximum_fusion.1
  76.0 15.4 %all-gather.1 = f32[1024,128]{1,0:T(8,128)S(1)} all-gather(f32[256,128]{1,0:T(8,128)S(1)} %pad_maximum_fusion.1), channel_id=3, replica_groups=mesh['x'=4,'z'=8,'col'=16] {'x'}, dimensions={0}, use_global_device_ids=true | all-gather | bytes 655360 | tf_op jit(solution)/shard_map/all_gather | solution.py:154
  91.5 0.0 all-to-all-done.3
  91.5 0.0 all-gather.4.cloned.1.call-done.panel_ref
  91.5 0.0 copy-done
  91.5 0.0 copy-done.1
  91.5 11.6 %finish.1 = (f32[2,128,128]{2,1,0:T(8,128)}, f32[2,2,16,128]{3,2,1,0:T(8,128)}, f32[2,1024,128]{2,1,0:T(8,128)}) custom-call(s32[2]{0:T(128)S(1)} %pad_add_fusion.place_ref, f32[4,8,32,128]{3,2,1,0:T(8,128)S(1)} %bitcast.120, f32[4,256,128]{2,1,0:T(8,128)S(1)} %bitcast.119, f32[2,128,1024]{2,1,0:T(8,128)S(1)} %copy-done, ...), custom_call_target="tpu_custom_call" | custom-call | tf_op jit(solution)/shard_map/finish/pallas_call | solution.py:118
  (11 shorter events, 0.1 us)
Async XLA Ops:
  7.2 84.3 %copy-start = (f32[2,128,1024]{2,1,0:T(8,128)S(1)}, f32[2,128,1024]{2,1,0:T(8,128)}, u32[]{:S(2)}) copy-start(f32[2,128,1024]{2,1,0:T(8,128)} %radiation_ref.1) | copy-start | bytes 3145732
  7.2 84.3 %copy-start.1 = (f32[2,1024,128]{2,1,0:T(8,128)S(1)}, f32[2,1024,128]{2,1,0:T(8,128)}, u32[]{:S(2)}) copy-start(f32[2,1024,128]{2,1,0:T(8,128)} %top_ref.1) | copy-start | bytes 3145732
  7.2 84.3 %all-gather.4.cloned.1.call-start = ((), (), s32[]{:S(2)}) async-start(), calls=%async_computation.4 | async-start | bytes 8912896 | tf_op jit(solution)/shard_map/all_gather | solution.py:138
  9.8 29.9 %all-to-all-start = ((f32[32,16,128]{2,1,0:T(8,128)}), f32[32,16,128]{2,1,0:T(8,128)S(1)}, u32[]{:S(2)}, u32[]{:S(2)}) async-start(f32[32,16,128]{2,1,0:T(8,128)} %bitcast.25), calls=%async_computation | async-start | bytes 524288 | tf_op jit(solution)/shard_map/all_to_all | solution.py:16
  71.5 20.0 %all-to-all-start.3 = ((f32[32,32,128]{2,1,0:T(8,128)}), f32[32,32,128]{2,1,0:T(8,128)S(1)}, u32[]{:S(2)}, u32[]{:S(2)}) async-start(f32[32,32,128]{2,1,0:T(8,128)} %broadcast_in_dim.33), calls=%async_computation.3 | async-start | bytes 1048576 | tf_op jit(solution)/shard_map/all_to_all | solution.py:16
Sparse Core Ops, SparseCore 0:
  10.1 60.7 all-gather.3
